TPU v7x, 128 devices: a whole 4x4x4 slice. The times are simulated.
128 devices in a mesh: seq: 4 (over y), kv: 32 (over z, x, core).
Axes of the slice: x: 4, y: 4, z: 4, core: 2. Of those that a mesh axis runs over, the one named last changes fastest.
Arguments:
- q_nope: bfloat16 [16, 8, 128, 128], P('seq', None, 'kv'), may hold values from -6 to 6
- q_rope: bfloat16 [16, 8, 128, 64], P('seq', None, 'kv')
- w_uk: bfloat16 [128, 128, 512], P('kv'), may hold values from -0.5 to 0.5
- w_uv: bfloat16 [128, 512, 128], P('kv'), may hold values from -0.25 to 0.25
- cache: bfloat16 [8192, 64, 576], P(('seq', 'kv'))
- page_table: int32 [16, 32, 16], P('seq', 'kv'), may hold values from 0 to 63, as said below
- lengths: int32 [16], P('seq'), may hold values from 2048 to 32768
- draft_kv: bfloat16 [16, 8, 576], P('seq'), may hold values from -6 to 6
- flags: int32 [16, 8], P('seq'), may hold values 0 or 1
Outputs:
- attended: bfloat16 [16, 8, 128, 128], P('seq', None, 'kv')
- accepted: int32 [16], P('seq')
- accepted_total: int32 [], replicated
Inputs may be any that keep to these rules, and one draw needn't show every extreme that they name: `page_table`: on every index of seq and kv, the 4 x 16 entries of the page table name each page of that device's pool exactly once.
All inputs are finite; a program needn't handle non-finite values. No bound on the sum of `flags` on one device may be relied on, other than what follows from the above.
Results may differ from a plain program's by a relative error of at most 0.019.
Values may be sent and summed in bfloat16 or wider, within the bound.
A program may use at most 128 MiB of HBM per device.

v0:
```python
import math

import jax
import jax.numpy as jnp
from jax import lax
from jax.sharding import Mesh
from jax.sharding import PartitionSpec as P

KV = ("kv_0", "kv_1", "kv_2")
SEQ_KV = ("seq", "kv_0", "kv_1", "kv_2")


def copy_for_each(array, axis):
    copies = jnp.broadcast_to(array, (lax.axis_size(axis), *array.shape))
    return lax.all_to_all(copies, axis, split_axis=0, concat_axis=0, tiled=True)


def of_everyone(array, axis):
    everything = copy_for_each(array, axis)
    return jnp.max(everything, axis=0)


def cut_along(array, dim, peers):
    before, after = (array.shape[:dim], array.shape[dim + 1 :])
    return jnp.moveaxis(array.reshape(*before, peers, -1, *after), dim, 0)


def sent_and_summed(array, axis, dim):
    peers = lax.axis_size(axis)
    tiles = lax.all_to_all(cut_along(array, dim, peers), axis, 0, 0, tiled=True)
    return jnp.sum(tiles.astype(jnp.float32), axis=0)


def sum_by_axis(array, axes, dim):
    far, near = axes
    own = sent_and_summed(cut_along(array, dim, lax.axis_size(far)), near, dim + 1)
    return jnp.sum(
        lax.all_to_all(own.astype(jnp.bfloat16), far, 0, 0, tiled=True).astype(jnp.float32), axis=0
    )


def side_by_side(arrays, axis, dim, along):
    widths = [math.prod(a.shape[along:]) for a in arrays]
    both = jnp.concatenate(
        [a.reshape(*a.shape[:along], w) for a, w in zip(arrays, widths)], axis=along
    )
    result = sum_by_axis(both, axis, dim)
    tiles = jnp.split(result, [sum(widths[:k]) for k in range(1, len(widths))], axis=along)
    return tuple(
        (b.reshape(*result.shape[:along], *a.shape[along:]) for a, b in zip(arrays, tiles))
    )


def over_copies(array, axis):
    everything = copy_for_each(array, axis)
    return jnp.sum(everything, axis=0)


def body(q_nope, q_rope, w_uk, w_uv, cache, page_table, lengths, draft_kv, flags):
    latent = w_uk.shape[2]
    heads_own = w_uk.shape[0]
    seq_count = q_nope.shape[0]
    drafts_count = q_nope.shape[1]
    width = cache.shape[2]
    scale = (q_nope.shape[-1] + q_rope.shape[-1]) ** (-0.5)
    q_lat = jnp.einsum("sihn,hnc->sihc", q_nope, w_uk, preferred_element_type=jnp.float32).astype(
        jnp.bfloat16
    )
    query_own = jnp.concatenate([q_lat, q_rope], axis=-1)
    query = lax.all_gather(query_own, KV, axis=2, tiled=True)
    heads_all = query.shape[2]
    rows = query.reshape(seq_count, drafts_count * heads_all, width)
    keys = cache[page_table[:, 0, :]]
    ctx_local = keys.shape[1] * keys.shape[2]
    keys = keys.reshape(seq_count, ctx_local, width)
    position = lax.axis_index(KV) * ctx_local + jnp.arange(ctx_local, dtype=jnp.int32)
    valid = (position[None, :] < lengths[:, None])[:, None, :]
    score = jnp.einsum("sqc,skc->sqk", rows, keys, preferred_element_type=jnp.float32) * scale
    score = jnp.where(valid, score, jnp.float32(-1e30))
    local_peak = jnp.max(score, axis=2)
    latent_keys = keys[:, :, :latent]
    head_start = lax.axis_index(KV) * heads_own
    peak = of_everyone(local_peak, KV)
    weight = jnp.where(valid, jnp.exp(score - peak[:, :, None]), jnp.float32(0.0))
    denom = jnp.sum(weight, axis=2).reshape(seq_count, drafts_count, heads_all)
    numer = jnp.einsum(
        "sqk,skc->sqc", weight.astype(jnp.bfloat16), latent_keys, preferred_element_type=jnp.float32
    )
    numer = numer.reshape(seq_count, drafts_count, heads_all, latent)
    numer_own, denom_own = side_by_side(
        (numer.astype(jnp.bfloat16), denom.astype(jnp.bfloat16)), (("kv_0", "kv_1"), "kv_2"), 2, 3
    )
    peak_own = lax.dynamic_slice_in_dim(
        peak.reshape(seq_count, drafts_count, heads_all), head_start, heads_own, 2
    )
    dscore = (
        jnp.einsum("sihc,sjc->sihj", query_own, draft_kv, preferred_element_type=jnp.float32)
        * scale
    )
    causal = (
        jnp.arange(drafts_count, dtype=jnp.int32)[None, :]
        <= jnp.arange(drafts_count, dtype=jnp.int32)[:, None]
    )[None, :, None, :]
    dpeak = jnp.max(jnp.where(causal, dscore, jnp.float32(-1e30)), axis=3)
    top = jnp.maximum(peak_own, dpeak)
    factor = jnp.exp(peak_own - top)
    dweight = jnp.where(causal, jnp.exp(dscore - top[..., None]), jnp.float32(0.0))
    total = denom_own * factor + jnp.sum(dweight, axis=3)
    mixed = numer_own * factor[..., None] + jnp.einsum(
        "sihj,sjc->sihc",
        dweight.astype(jnp.bfloat16),
        draft_kv[:, :, :latent],
        preferred_element_type=jnp.float32,
    )
    latent_out = (mixed / total[..., None]).astype(jnp.bfloat16)
    attended = jnp.einsum(
        "sihc,hcv->sihv", latent_out, w_uv, preferred_element_type=jnp.float32
    ).astype(jnp.bfloat16)
    accepted = jnp.sum(jnp.cumprod(flags, axis=1), axis=1)
    accepted_total = over_copies(jnp.sum(accepted), "seq")
    return (attended, accepted, accepted_total)


def solution(mesh):
    split = Mesh(mesh.devices.reshape(mesh.shape["seq"], 4, 4, 2), ("seq", "kv_0", "kv_1", "kv_2"))
    return jax.shard_map(
        body,
        mesh=split,
        in_specs=(
            P("seq", None, KV, None),
            P("seq", None, KV, None),
            P(KV, None, None),
            P(KV, None, None),
            P(SEQ_KV, None, None),
            P("seq", KV, None),
            P("seq"),
            P("seq", None, None),
            P("seq", None),
        ),
        out_specs=(P("seq", None, KV, None), P("seq"), P()),
        check_vma=False,
    )
```

profile of v0, /device:TPU:0, one launch (start us, length us, event | category | flops | bytes accessed | tf_op | source)
XLA Modules:
  0.0 223.7 jit_solution(2933034135864817126)
XLA Ops:
  8.2 0.9 fusion.19
  10.7 6.0 %gather_fusion = bf16[64,64,576]{2,1,0:T(8,128)(2,1)} fusion(bf16[64,64,576]{2,1,0:T(8,128)(2,1)} %param.13, s32[1024]{0:T(1024)S(1)} %pad_clamp_fusion), kind=kCustom, calls=%fused_computation | custom fusion | bytes 9437440 | tf_op jit(solution)/shard_map/gather | solution.py:73
  16.8 43.4 %all-gather.2.cloned.1.call-done = bf16[4,8,128,576]{3,1,0,2:T(8,128)(2,1)} async-done(((bf16[4,8,4,576]{3,1,0,2:T(8,128)(2,1)}), bf16[4,8,128,576]{3,1,0,2:T(8,128)(2,1)}) %all-gather.2.cloned.1.call-update) | async-done | bytes 4718608 | tf_op jit(solution)/shard_map/all_gather | solution.py:70
  60.1 9.2 %copy.116 = bf16[4,8,128,576]{2,1,3,0:T(8,128)(2,1)} copy(bf16[4,8,128,576]{3,1,0,2:T(8,128)(2,1)} %all-gather.2.cloned.1.call-done) | data formatting | bytes 9437184 | tf_op jit(solution)/shard_map/all_gather | solution.py:70
  69.4 8.2 %reshape.114 = bf16[4,1024,576]{1,2,0:T(8,128)(2,1)} reshape(bf16[4,8,128,576]{2,1,3,0:T(8,128)(2,1)} %copy.116) | data formatting | bytes 9437184 | tf_op jit(solution)/shard_map/reshape | solution.py:72
  77.5 13.8 %fusion = (f32[4,1024]{1,0:T(4,128)S(1)}, f32[4,1024,1024]{1,2,0:T(8,128)}) fusion(pred[4,1024]{1,0:T(4,128)(4,1)S(1)} %broadcast_compare_fusion, bf16[4,1024,576]{2,1,0:T(8,128)(2,1)} %bitcast.58, bf16[4,1024,576]{1,2,0:T(8,128)(2,1)} %reshape.114), kind=kOutput, calls=%fused_computation.3 | convolution fusion | flops 4844417024 | bytes 26234880 | tf_op jit(solution)/shard_map/sqc,skc->sqk/dot_general | solution.py:78
  91.4 0.9 broadcast_in_dim.57
  92.3 5.0 %all-to-all-start = ((f32[32,4,1024]{2,1,0:T(4,128)}), f32[32,4,1024]{2,1,0:T(4,128)S(1)}, u32[]{:S(2)}, u32[]{:S(2)}) async-start(f32[32,4,1024]{2,1,0:T(4,128)} %broadcast_in_dim.57), calls=%async_computation | async-start | bytes 1048576 | tf_op jit(solution)/shard_map/all_to_all | solution.py:15
  98.2 10.7 %all-to-all-done = f32[32,4,1024]{2,1,0:T(4,128)S(1)} async-done(((f32[32,4,1024]{2,1,0:T(4,128)}), f32[32,4,1024]{2,1,0:T(4,128)S(1)}, u32[]{:S(2)}, u32[]{:S(2)}) %all-to-all-start) | async-done | bytes 524320 | tf_op jit(solution)/shard_map/all_to_all | solution.py:15
  109.0 10.9 %fusion.11 = bf16[4,1024,512]{2,1,0:T(8,128)(2,1)S(1)} fusion(bf16[4,1024,576]{2,1,0:T(8,128)(2,1)} %bitcast.59, f32[4,1024,1024]{1,2,0:T(8,128)} %get-tuple-element.32, f32[4,1024]{1,0:T(4,128)S(1)} %reduce_max.28, pred[4,1024]{1,0:T(4,128)(4,1)S(1)} %broadcast_compare_fusion), kind=kOutput, calls=%fused_computation.15 | convolution fusion | flops 4318035968 | bytes 25186304 | tf_op jit(solution)/shard_map/sqk,skc->sqc/dot_general | solution.py:86
  119.9 8.2 %fusion.1 = bf16[4,1024]{1,0:T(4,128)(2,1)S(1)} fusion(f32[4,1024,1024]{1,2,0:T(8,128)} %get-tuple-element.32, f32[4,1024]{1,0:T(4,128)S(1)} %reduce_max.28, pred[4,1024]{1,0:T(4,128)(4,1)S(1)} %broadcast_compare_fusion), kind=kLoop, calls=%fused_computation.4 | loop fusion | flops 20967424 | bytes 16805888 | tf_op jit(solution)/shard_map/reduce_sum | solution.py:85
  128.1 6.4 %copy.120 = bf16[4,8,16,8,512]{4,1,3,0,2:T(8,128)(2,1)} copy(bf16[4,8,16,8,512]{4,3,2,1,0:T(8,128)(2,1)S(1)} %bitcast.60) | data formatting | bytes 8388608 | tf_op jit(solution)/shard_map/convert_element_type | solution.py:91
  134.8 3.1 %copy.121 = bf16[4,8,16,8,1]{4,1,3,0,2:T(8,128)(2,1)S(1)} copy(bf16[4,8,16,8,1]{3,2,1,0,4:T(8,128)(2,1)S(1)} %convert_element_type.53) | data formatting | bytes 16384 | tf_op jit(solution)/shard_map/convert_element_type | solution.py:91
  137.9 3.0 %pad_maximum_fusion = bf16[4,8,16,8,513]{4,1,3,0,2:T(8,128)(2,1)S(1)} fusion(bf16[4,8,16,8,1]{4,1,3,0,2:T(8,128)(2,1)S(1)} %copy.121, bf16[4,8,16,8,512]{4,1,3,0,2:T(8,128)(2,1)} %copy.120), kind=kLoop, calls=%fused_computation.12 | loop fusion | flops 8404992 | bytes 8404992 | tf_op jit(solution)/shard_map/concatenate | solution.py:44
  140.9 3.0 %copy.122 = bf16[2,16,4,8,4,513]{5,4,1,3,2,0:T(4,128)(2,1)S(1)} copy(bf16[2,16,4,8,4,513]{5,3,4,0,2,1:T(8,128)(2,1)S(1)} %bitcast.57) | data formatting | bytes 8404992 | tf_op jit(solution)/shard_map/transpose | solution.py:25
  143.9 9.1 %all_to_all.21 = bf16[2,16,4,8,4,513]{5,4,1,3,2,0:T(4,128)(2,1)} all-to-all(bf16[2,16,4,8,4,513]{5,4,1,3,2,0:T(4,128)(2,1)S(1)} %copy.122), channel_id=1, replica_groups=mesh['seq'=4,'kv_0'=4,'kv_1'=4,'kv_2'=2] {'kv_2'}, dimensions={0} | all-to-all | bytes 8404992 | tf_op jit(solution)/shard_map/all_to_all | solution.py:30
  152.9 1.2 broadcast_in_dim.62
  154.2 4.3 %all-to-all-start.3 = ((s32[4,1,1]{2,1,0:T(1,128)}), s32[4,1,1]{2,1,0:T(1,128)S(1)}, u32[]{:S(2)}, u32[]{:S(2)}) async-start(s32[4,1,1]{2,1,0:T(1,128)} %broadcast_in_dim.62), calls=%async_computation.3 | async-start | bytes 4096 | tf_op jit(solution)/shard_map/all_to_all | solution.py:15
  158.5 7.2 %reduce_sum.67 = bf16[16,4,8,4,513]{4,3,0,2,1:T(4,128)(2,1)S(1)} reduce(bf16[2,16,4,8,4,513]{5,4,1,3,2,0:T(4,128)(2,1)} %all_to_all.21, bf16[]{:T(256)} %constant.37.clone.1), dimensions={0}, to_apply=%region_3.4 | reduce | flops 1050624 | bytes 6303746 | tf_op jit(solution)/shard_map/reduce_sum | solution.py:31
  165.7 2.8 %copy.124 = bf16[16,4,8,4,513]{4,3,2,1,0:T(4,128)(2,1)} copy(bf16[16,4,8,4,513]{4,3,0,2,1:T(4,128)(2,1)S(1)} %reduce_sum.67) | data formatting | bytes 4202496 | tf_op jit(solution)/shard_map/reduce_sum | solution.py:31
  168.5 3.7 %all-to-all-start.2 = ((bf16[16,4,8,4,513]{4,3,2,1,0:T(4,128)(2,1)}), bf16[16,4,8,4,513]{4,3,2,1,0:T(4,128)(2,1)S(1)}, u32[]{:S(2)}, u32[]{:S(2)}) async-start(bf16[16,4,8,4,513]{4,3,2,1,0:T(4,128)(2,1)} %copy.124), calls=%async_computation.2 | async-start | bytes 5242880 | tf_op jit(solution)/shard_map/all_to_all | solution.py:38
  174.3 38.5 %all-to-all-done.2 = bf16[16,4,8,4,513]{4,3,2,1,0:T(4,128)(2,1)S(1)} async-done(((bf16[16,4,8,4,513]{4,3,2,1,0:T(4,128)(2,1)}), bf16[16,4,8,4,513]{4,3,2,1,0:T(4,128)(2,1)S(1)}, u32[]{:S(2)}, u32[]{:S(2)}) %all-to-all-start.2) | async-done | bytes 2101280 | tf_op jit(solution)/shard_map/all_to_all | solution.py:38
  213.9 1.0 fusion.17
  214.9 1.2 fusion.20
  (41 shorter events, 7.6 us)
Async XLA Ops:
  7.2 1.1 copy-start
  7.2 52.9 %all-gather.2.cloned.1.call-start = ((), (), s32[]{:S(2)}) async-start(), calls=%async_computation.4 | async-start | bytes 5406720 | tf_op jit(solution)/shard_map/all_gather | solution.py:70
  10.7 6.0 %copy-start.5 = (s32[4]{0:T(128)S(1)}, s32[4]{0:T(128)}, u32[]{:S(2)}) copy-start(s32[4]{0:T(128)} %param.15) | copy-start | bytes 52
  77.5 19.8 %copy-start.3 = (s32[4,8]{1,0:T(4,128)S(1)}, s32[4,8]{1,0:T(4,128)}, u32[]{:S(2)}) copy-start(s32[4,8]{1,0:T(4,128)} %param.17) | copy-start | bytes 388
  92.3 16.6 %all-to-all-start = ((f32[32,4,1024]{2,1,0:T(4,128)}), f32[32,4,1024]{2,1,0:T(4,128)S(1)}, u32[]{:S(2)}, u32[]{:S(2)}) async-start(f32[32,4,1024]{2,1,0:T(4,128)} %broadcast_in_dim.57), calls=%async_computation | async-start | bytes 1048576 | tf_op jit(solution)/shard_map/all_to_all | solution.py:15
  154.2 14.3 %all-to-all-start.3 = ((s32[4,1,1]{2,1,0:T(1,128)}), s32[4,1,1]{2,1,0:T(1,128)S(1)}, u32[]{:S(2)}, u32[]{:S(2)}) async-start(s32[4,1,1]{2,1,0:T(1,128)} %broadcast_in_dim.62), calls=%async_computation.3 | async-start | bytes 4096 | tf_op jit(solution)/shard_map/all_to_all | solution.py:15
  165.7 6.6 %copy-start.2 = (bf16[4,8,4,576]{3,1,0,2:T(8,128)(2,1)S(1)}, bf16[4,8,4,576]{3,1,0,2:T(8,128)(2,1)}, u32[]{:S(2)}) copy-start(bf16[4,8,4,576]{3,1,0,2:T(8,128)(2,1)} %pad_maximum_fusion.1) | copy-start | bytes 442372
  165.7 6.6 %copy-start.6 = (bf16[4,8,576]{2,1,0:T(8,128)(2,1)S(1)}, bf16[4,8,576]{2,1,0:T(8,128)(2,1)}, u32[]{:S(2)}) copy-start(bf16[4,8,576]{2,1,0:T(8,128)(2,1)} %param.16) | copy-start | bytes 110596
  165.7 51.1 %copy-start.1 = (bf16[4,128,512]{2,1,0:T(8,128)(2,1)S(1)}, bf16[4,128,512]{2,1,0:T(8,128)(2,1)}, u32[]{:S(2)}) copy-start(bf16[4,128,512]{2,1,0:T(8,128)(2,1)} %param.11) | copy-start | bytes 1572868
  168.5 44.3 %all-to-all-start.2 = ((bf16[16,4,8,4,513]{4,3,2,1,0:T(4,128)(2,1)}), bf16[16,4,8,4,513]{4,3,2,1,0:T(4,128)(2,1)S(1)}, u32[]{:S(2)}, u32[]{:S(2)}) async-start(bf16[16,4,8,4,513]{4,3,2,1,0:T(4,128)(2,1)} %copy.124), calls=%async_computation.2 | async-start | bytes 5242880 | tf_op jit(solution)/shard_map/all_to_all | solution.py:38
  172.2 2.0 copy-start.4
Sparse Core Ops, SparseCore 0:
  10.2 49.8 all-gather.1
where the time goes:
time: 225 us; the launch traced here: 224 us
  waiting for transfers between devices  92.6 us (41%)
  local copies, waits for them, and re-layouts  43.1 us (19%)
  matrix products  28.5 us (13%)
  other arithmetic  23.1 us (10%)
  between operations  14.2 us (6%)
  starting transfers between devices  13.1 us (6%)
  blocking collectives  9.08 us (4%)
    all_gather x1, waiting for transfers between devices, body(): query = lax.all_gather(query_own, KV, axis=2, tiled=True)  43.4 us
    all_to_all x1, waiting for transfers between devices, sum_by_axis(): lax.all_to_all(own.astype(jnp.bfloat16), far, 0, 0, tiled=True)  38.5 us
    dot_general x1, matrix products, body(): jnp.einsum('sqc,skc->sqk', rows, keys, preferred_element_type=jnp.float32)  13.8 us
    dot_general x1, matrix products, body(): jnp.einsum('sqk,skc->sqc', weight.astype(jnp.bfloat16), latent_keys, pref...  10.9 us
    all_to_all x2, waiting for transfers between devices, copy_for_each(): return lax.all_to_all(copies, axis, split_axis=0, concat_axis=0, tiled=True)  10.7 us
    all_to_all x2, starting transfers between devices, copy_for_each(): return lax.all_to_all(copies, axis, split_axis=0, concat_axis=0, tiled=True)  9.32 us
    all_gather x1, local copies, waits for them, and re-layouts, body(): query = lax.all_gather(query_own, KV, axis=2, tiled=True)  9.25 us
    all_to_all x1, blocking collectives, sent_and_summed(): tiles = lax.all_to_all(cut_along(array, dim, peers), axis, 0, 0, tiled=True)  9.08 us
  transfers between devices with their start and end apart: 4, of which 3 were waited for; matrix products, arithmetic and copies ran while one was open for 9% of the time, Pallas kernels for 0%

commit v1 on v0

v1 whole, which is shorter than its diff:
```python
import functools
import math

import jax
import jax.numpy as jnp
from jax import lax
from jax.experimental import pallas as pl
from jax.experimental.pallas import tpu as pltpu
from jax.sharding import Mesh
from jax.sharding import PartitionSpec as P

KV = ("kv_0", "kv_1", "kv_2")
SEQ_KV = ("seq", "kv_0", "kv_1", "kv_2")
AXES = (("kv_1", "kv_0"), ("kv_0", "kv_1"))
POS = (0, 1, 3, 2)
GROUPS = ((0, 1), (1, 2), (3, 1))
RING = 4
MASKED = -1e30
MESH = pl.DeviceIdType.MESH
NT = (((1,), (1,)), ((), ()))
NN = (((1,), (0,)), ((), ()))


def dot(a, b, dims=NN):
    return lax.dot_general(a, b, dims, preferred_element_type=jnp.float32)


def shifted(axis, by):
    return {axis: lax.rem(lax.axis_index(axis) + by, RING)}


def kernel(
    scale,
    qn_hbm, qr_hbm, wuk_hbm, wuv_hbm, cache_hbm, draft_hbm, pt_ref, len_ref, flags_ref,
    out_ref, acc_ref, tot_ref,
    qn, qr, wuk, wuv, pool, draft, kbuf, qbuf, nsend, nrecv, ssend, srecv,
    csend, crecv, tsend, trecv, nd, md, ld, lo, count, counts,
    in_sem, key_s, key_r, q1_s, q1_r, q2_s, q2_r, n_s, n_r, s_s, s_r, c_s, c_r, t_s, t_r,
    a_s, a_r,
):
    rate = scale * math.log2(math.e)
    rows = qbuf.shape[3]
    latent = nsend.shape[5]
    seqs, ctx = kbuf.shape[0], kbuf.shape[1]
    own_ctx = ctx // 2
    pages, page = pt_ref.shape[2], pool.shape[1]
    heads = wuk.shape[0]
    line = RING * rows
    core = lax.axis_index("kv_2")
    chip = lax.axis_index("kv_0") * RING + lax.axis_index("kv_1")
    partner = {"kv_2": 1 - core}

    small = []
    for i, (src, dst) in enumerate(
        ((qn_hbm, qn), (wuk_hbm, wuk), (qr_hbm, qr), (draft_hbm, draft), (wuv_hbm, wuv))
    ):
        small.append(pltpu.make_async_copy(src, dst, in_sem.at[i]))
    for copy in small[:4]:
        copy.start()
    quarter = pool.shape[0] // 4
    pools = []
    for i in range(4):
        part = pl.ds(i * quarter, quarter)
        pools.append(pltpu.make_async_copy(cache_hbm.at[part], pool.at[part], in_sem.at[5 + i]))
        pools[-1].start()
    small[4].start()

    barrier = pltpu.get_barrier_semaphore()
    peers = [partner] + [
        shifted(axis, by) for axis in ("kv_0", "kv_1", "seq") for by in range(1, RING)
    ]
    for peer in peers:
        pl.semaphore_signal(barrier, inc=1, device_id=peer, device_id_type=MESH)

    def remote(src, dst, send, recv, peer):
        return pltpu.make_async_remote_copy(
            src_ref=src, dst_ref=dst, send_sem=send, recv_sem=recv,
            device_id=peer, device_id_type=MESH,
        )

    mine = jnp.int32(0)
    for s in range(seqs):
        run, total = jnp.int32(1), jnp.int32(0)
        for i in range(flags_ref.shape[1]):
            run = run * flags_ref[s, i]
            total = total + run
        acc_ref[s] = total
        mine = mine + total
    count[...] = jnp.full(count.shape, mine, jnp.int32)

    for copy in small[:4]:
        copy.wait()
    row = lax.broadcasted_iota(jnp.int32, qn.shape, 0)
    qn_f = qn[...].astype(jnp.float32)
    q_lat = jnp.zeros((qn.shape[0], latent), jnp.float32)
    for h in range(heads):
        part = jnp.where(lax.rem(row, heads) == h, qn_f, 0.0).astype(jnp.bfloat16)
        q_lat = q_lat + dot(part, wuk[h])
    q_lat = q_lat.astype(jnp.bfloat16)
    for s in range(seqs):
        h, u = s // 2, s % 2
        qbuf[h, 0, 0, :, u * latent:(u + 1) * latent] = q_lat[s * rows:(s + 1) * rows]
    for h in range(2):
        ropes = [qr[(2 * h + u) * rows:(2 * h + u + 1) * rows] for u in range(2)]
        qbuf[h, 0, 0, :, 2 * latent:] = jnp.concatenate(ropes, axis=1)

    keys_d = draft[:, :latent]
    d_score = dot(q_lat, keys_d, NT) + dot(qr[...], draft[:, latent:], NT)
    per_seq, drafts = qn.shape[0] // seqs, draft.shape[0] // seqs
    r = lax.broadcasted_iota(jnp.int32, d_score.shape, 0)
    c = lax.broadcasted_iota(jnp.int32, d_score.shape, 1)
    seen = (r // per_seq == c // drafts) & (lax.rem(c, drafts) <= lax.rem(r, per_seq) // heads)
    d_score = jnp.where(seen, d_score, MASKED)
    d_top = jnp.max(d_score, axis=1, keepdims=True)
    d_w = jnp.where(seen, jnp.exp2((d_score - d_top) * rate), 0.0)
    md[...] = jnp.broadcast_to(d_top, md.shape)
    ld[...] = jnp.broadcast_to(jnp.sum(d_w, axis=1, keepdims=True), ld.shape)
    nd[...] = dot(d_w.astype(jnp.bfloat16), keys_d)

    pl.semaphore_wait(barrier, len(peers))

    started = []

    def stage_one(h, by):
        copy = remote(
            qbuf.at[h, 0, 0], qbuf.at[h, 0, RING - by], q1_s.at[h, by - 1],
            q1_r.at[h, RING - by - 1], shifted(AXES[h][0], by),
        )
        copy.start()
        started.append(copy)

    def stage_two(h, j, by):
        copy = remote(
            qbuf.at[h, 0, j], qbuf.at[h, POS[RING - by], j], q2_s.at[h, by - 1, j],
            q2_r.at[h, RING - by - 1, j], shifted(AXES[h][1], by),
        )
        copy.start()
        started.append(copy)

    for by in (1, 3, 2):
        for h in range(2):
            stage_one(h, by)
    for by in (3, 1):
        for h in range(2):
            stage_two(h, 0, by)
    tallies = []
    for by in range(1, RING):
        copy = remote(
            count, counts.at[RING - by - 1], a_s.at[by - 1], a_r.at[RING - by - 1],
            shifted("seq", by),
        )
        copy.start()
        tallies.append(copy)

    for copy in pools:
        copy.wait()
    key_copies = []

    def send_keys(s):
        part = pl.ds(core * own_ctx, own_ctx)
        copy = remote(kbuf.at[s, part], kbuf.at[s, part], key_s.at[s], key_r.at[s], partner)
        copy.start()
        key_copies.append(copy)

    for s in range(seqs):
        def place(t, _, s=s):
            tokens = pool[pt_ref[s, 0, t]]
            at = pl.ds(pl.multiple_of(core * own_ctx + t * page, page), page)
            kbuf[s, at, :latent] = tokens[:, :latent]
            rope = tokens[:, latent:]
            none = jnp.zeros_like(rope)
            both = [rope, none] if s % 2 == 0 else [none, rope]
            kbuf[s, at, latent:] = jnp.concatenate(both, axis=1)
            return 0

        lax.fori_loop(0, pages, place, 0)
        if s:
            send_keys(s - 1)

    for j in (1, 3, 2):
        for h in range(2):
            remote(
                qbuf.at[h, 0, j], qbuf.at[h, 0, j], q1_s.at[h, 0], q1_r.at[h, j - 1],
                partner,
            ).wait_recv()
            for by in (3, 1):
                stage_two(h, j, by)
    send_keys(seqs - 1)
    for j in range(RING):
        for h in range(2):
            stage_two(h, j, 2)

    heavy = []

    def compute(h, group):
        first, places = group
        height = places * line
        for place in range(first, first + places):
            slot = POS[place]
            if slot:
                for j in range(RING):
                    dst = qbuf.at[h, place, j]
                    remote(
                        dst, dst, q2_s.at[h, 0, j], q2_r.at[h, slot - 1, j], partner
                    ).wait_recv()

        def one(u, _):
            s = 2 * h + u
            at = pl.ds(pl.multiple_of(u * latent, latent), latent)
            q = qbuf[h, first:first + places, :, :, at].reshape(height, latent)
            qrope = qbuf[h, first:first + places, :, :, 2 * latent:].reshape(height, 128)
            score = dot(q, kbuf[s, :, :latent], NT) + dot(qrope, kbuf[s, :, latent:], NT)
            position = chip * ctx + lax.broadcasted_iota(jnp.int32, (1, ctx), 1)
            valid = position < len_ref[s]
            score = jnp.where(valid, score, MASKED)
            top = jnp.max(score, axis=1, keepdims=True)
            weight = jnp.where(valid, jnp.exp2((score - top) * rate), 0.0)
            total = jnp.sum(weight, axis=1, keepdims=True)
            lane = lax.broadcasted_iota(jnp.int32, (height, 128), 1)
            stats = jnp.transpose(jnp.where(lane == 0, top, total))[:8]
            for k in range(places):
                ssend[h, first + k, u] = stats[:, k * line:(k + 1) * line]
            numer = dot(weight.astype(jnp.bfloat16), kbuf[s, :, :latent])
            numer = numer.astype(jnp.bfloat16).reshape(places, RING, rows, latent)
            nsend[h, first:first + places, :, u] = numer
            return 0

        lax.fori_loop(0, 2, one, 0)
        for place in range(first, first + places):
            slot = POS[place]
            if slot:
                copies = (
                    remote(
                        nsend.at[h, place], nrecv.at[h, RING - slot - 1], n_s.at[h, slot - 1],
                        n_r.at[h, RING - slot - 1], shifted(AXES[h][1], slot),
                    ),
                    remote(
                        ssend.at[h, place], srecv.at[h, RING - slot - 1], s_s.at[h, slot - 1],
                        s_r.at[h, RING - slot - 1], shifted(AXES[h][1], slot),
                    ),
                )
                for copy in copies:
                    copy.start()
                    heavy.append(copy)

    def keys_arrived(s):
        part = pl.ds((1 - core) * own_ctx, own_ctx)
        remote(
            kbuf.at[s, part], kbuf.at[s, part], key_s.at[s], key_r.at[s], partner
        ).wait_recv()

    for g, group in enumerate(GROUPS):
        for h in range(2):
            if g == 0:
                keys_arrived(2 * h)
                keys_arrived(2 * h + 1)
            compute(h, group)

    light = []
    for h in range(2):
        for slot in range(1, RING):
            remote(
                nrecv.at[h, slot - 1], nrecv.at[h, slot - 1], n_s.at[h, 0], n_r.at[h, slot - 1],
                partner,
            ).wait_recv()
            remote(
                srecv.at[h, slot - 1], srecv.at[h, slot - 1], s_s.at[h, 0], s_r.at[h, slot - 1],
                partner,
            ).wait_recv()
        for u in range(2):
            stat = [ssend[h, 0, u]] + [srecv[h, k, u] for k in range(RING - 1)]
            tops = [x[0:1] for x in stat]
            top = functools.reduce(jnp.maximum, tops)
            ws = [jnp.exp2((x - top) * rate) for x in tops]
            total = sum(w * x[1:2] for w, x in zip(ws, stat))
            sub = lax.broadcasted_iota(jnp.int32, (8, line), 0)
            tsend[h, u] = jnp.where(sub == 0, top, total)
            pick = ws[3]
            for k in (2, 1, 0):
                pick = jnp.where(sub == k, ws[k], pick)
            cols = jnp.transpose(pick)
            mixed = jnp.zeros((line, latent), jnp.float32)
            for k in range(RING):
                part = nsend[h, 0, :, u] if k == 0 else nrecv[h, k - 1, :, u]
                part = part.reshape(line, latent).astype(jnp.float32)
                mixed = mixed + cols[:, k:k + 1] * part
            csend[h, :, u] = mixed.astype(jnp.bfloat16).reshape(RING, rows, latent)
        for j in (1, 3, 2):
            copies = (
                remote(
                    csend.at[h, j], crecv.at[h, RING - j - 1], c_s.at[h, j - 1],
                    c_r.at[h, RING - j - 1], shifted(AXES[h][0], j),
                ),
                remote(
                    tsend.at[h], trecv.at[h, RING - j - 1], t_s.at[h, j - 1],
                    t_r.at[h, RING - j - 1], shifted(AXES[h][0], j),
                ),
            )
            for copy in copies:
                copy.start()
                light.append(copy)

    for h in range(2):
        for slot in range(1, RING):
            remote(
                crecv.at[h, slot - 1], crecv.at[h, slot - 1], c_s.at[h, 0], c_r.at[h, slot - 1],
                partner,
            ).wait_recv()
            remote(
                trecv.at[h, slot - 1], trecv.at[h, slot - 1], t_s.at[h, 0], t_r.at[h, slot - 1],
                partner,
            ).wait_recv()
        for u in range(2):
            here = pl.ds((2 * h + u) * rows, rows)
            tops, totals, parts = [md[here, 0:1]], [ld[here, 0:1]], [nd[here]]
            for slot in range(RING):
                j = (RING - slot) % RING
                stat = tsend[h, u] if slot == 0 else trecv[h, slot - 1, u]
                cols = jnp.transpose(stat)[j * rows:(j + 1) * rows]
                tops.append(cols[:, 0:1])
                totals.append(cols[:, 1:2])
                part = csend[h, 0, u] if slot == 0 else crecv[h, slot - 1, u]
                parts.append(part.astype(jnp.float32))
            top = functools.reduce(jnp.maximum, tops)
            ws = [jnp.exp2((x - top) * rate) for x in tops]
            total = sum(w * x for w, x in zip(ws, totals))
            mixed = sum(w * x for w, x in zip(ws, parts))
            lo[here] = (mixed / total).astype(jnp.bfloat16)

    small[4].wait()
    latent_out = lo[...]
    attended = jnp.zeros(out_ref.shape, jnp.float32)
    row = lax.broadcasted_iota(jnp.int32, out_ref.shape, 0)
    for h in range(heads):
        attended = jnp.where(lax.rem(row, heads) == h, dot(latent_out, wuv[h]), attended)
    out_ref[...] = attended.astype(out_ref.dtype)

    for copy in tallies:
        copy.wait_recv()
    everyone = count[...] + counts[0] + counts[1] + counts[2]
    tot_ref[...] = everyone
    for copy in tallies + started + key_copies + heavy + light:
        copy.wait_send()


def body(q_nope, q_rope, w_uk, w_uv, cache, page_table, lengths, draft_kv, flags):
    seqs, drafts, heads, nope = q_nope.shape
    latent, width = w_uk.shape[2], cache.shape[2]
    rope = width - latent
    scale = (nope + rope) ** -0.5
    count = seqs * drafts * heads
    rows = drafts * heads
    ctx = 2 * page_table.shape[2] * cache.shape[1]
    bf16, f32 = jnp.bfloat16, jnp.float32
    hbm = pl.BlockSpec(memory_space=pl.ANY)
    smem = pl.BlockSpec(memory_space=pltpu.SMEM)
    vmem = pl.BlockSpec(memory_space=pltpu.VMEM)
    dma = pltpu.SemaphoreType.DMA
    scratch = [
        pltpu.VMEM((count, nope), bf16),
        pltpu.VMEM((count, rope), bf16),
        pltpu.VMEM(w_uk.shape, bf16),
        pltpu.VMEM(w_uv.shape, bf16),
        pltpu.VMEM(cache.shape, bf16),
        pltpu.VMEM((seqs * drafts, width), bf16),
        pltpu.VMEM((seqs, ctx, latent + 2 * rope), bf16),
        pltpu.VMEM((2, RING, RING, rows, 2 * (latent + rope)), bf16),
        pltpu.VMEM((2, RING, RING, 2, rows, latent), bf16),
        pltpu.VMEM((2, RING - 1, RING, 2, rows, latent), bf16),
        pltpu.VMEM((2, RING, 2, 8, RING * rows), f32),
        pltpu.VMEM((2, RING - 1, 2, 8, RING * rows), f32),
        pltpu.VMEM((2, RING, 2, rows, latent), bf16),
        pltpu.VMEM((2, RING - 1, 2, rows, latent), bf16),
        pltpu.VMEM((2, 2, 8, RING * rows), f32),
        pltpu.VMEM((2, RING - 1, 2, 8, RING * rows), f32),
        pltpu.VMEM((count, latent), f32),
        pltpu.VMEM((count, 128), f32),
        pltpu.VMEM((count, 128), f32),
        pltpu.VMEM((count, latent), bf16),
        pltpu.VMEM((8, 128), jnp.int32),
        pltpu.VMEM((RING - 1, 8, 128), jnp.int32),
        dma((9,)),
        dma((seqs,)), dma((seqs,)),
        dma((2, RING - 1)), dma((2, RING - 1)),
        dma((2, RING - 1, RING)), dma((2, RING - 1, RING)),
        dma((2, RING - 1)), dma((2, RING - 1)),
        dma((2, RING - 1)), dma((2, RING - 1)),
        dma((2, RING - 1)), dma((2, RING - 1)),
        dma((2, RING - 1)), dma((2, RING - 1)),
        dma((RING - 1,)), dma((RING - 1,)),
    ]
    attended, accepted, total = pl.pallas_call(
        functools.partial(kernel, scale),
        out_shape=(
            jax.ShapeDtypeStruct((count, w_uv.shape[2]), bf16),
            jax.ShapeDtypeStruct((seqs,), jnp.int32),
            jax.ShapeDtypeStruct((8, 128), jnp.int32),
        ),
        in_specs=[hbm] * 6 + [smem] * 3,
        out_specs=(vmem, smem, vmem),
        scratch_shapes=scratch,
        compiler_params=pltpu.CompilerParams(
            collective_id=0, has_side_effects=True, vmem_limit_bytes=60 * 1024 * 1024
        ),
        name="verify",
    )(
        q_nope.reshape(count, nope),
        q_rope.reshape(count, rope),
        w_uk,
        w_uv,
        cache,
        draft_kv.reshape(seqs * drafts, width),
        page_table,
        lengths,
        flags,
    )
    return attended.reshape(seqs, drafts, heads, -1), accepted, total[0, 0]


def solution(mesh):
    split = Mesh(mesh.devices.reshape(mesh.shape["seq"], RING, RING, 2), SEQ_KV)
    return jax.shard_map(
        body,
        mesh=split,
        in_specs=(
            P("seq", None, KV, None),
            P("seq", None, KV, None),
            P(KV, None, None),
            P(KV, None, None),
            P(SEQ_KV, None, None),
            P("seq", KV, None),
            P("seq"),
            P("seq", None, None),
            P("seq", None),
        ),
        out_specs=(P("seq", None, KV, None), P("seq"), P()),
        check_vma=False,
    )
```

time: 225 us -> 58.3 us (0.26)
  waiting for transfers between devices: 92.6 us -> 0 us
  Pallas kernels: 0 us -> 52.9 us
  local copies, waits for them, and re-layouts: 43.1 us -> 3.72 us
  matrix products: 28.5 us -> 0 us
  other arithmetic: 23.1 us -> 0 us
  between operations: 14.2 us -> 0.64 us
  starting transfers between devices: 13.1 us -> 0 us
  blocking collectives: 9.08 us -> 0 us
    pallas_call x0 -> x1, Pallas kernels: none -> 52.9 us  [body(): pl.pallas_call(functools.partial(kernel, scale), out_shape=(jax.ShapeDtyp...]
    all_to_all x3 -> x0, waiting for transfers between devices: 49.2 us -> none  [the longest x1 38.5 us: sum_by_axis(): lax.all_to_all(own.astype(jnp.bfloat16), far, 0, 0, tiled=True)]
    all_gather x1 -> x0, waiting for transfers between devices: 43.4 us -> none  [body(): query = lax.all_gather(query_own, KV, axis=2, tiled=True)]
    dot_general x5 -> x0, matrix products: 27.5 us -> none  [the longest x1 13.8 us: body(): jnp.einsum('sqc,skc->sqk', rows, keys, preferred_element_type=jnp.float32)]
    reduce_sum x6 -> x0, other arithmetic: 17.6 us -> none  [the longest x1 8.19 us: body(): denom = jnp.sum(weight, axis=2).reshape(seq_count, drafts_count, heads_all)]
    all_to_all x3 -> x0, starting transfers between devices: 13.1 us -> none  [the longest x2 9.32 us: copy_for_each(): return lax.all_to_all(copies, axis, split_axis=0, concat_axis=0, tiled=True)]
    convert_element_type x3 -> x0, local copies, waits for them, and re-layouts: 9.7 us -> none  [the longest x1 6.44 us: body(): numer.astype(jnp.bfloat16)]
    all_gather x1 -> x0, local copies, waits for them, and re-layouts: 9.25 us -> none  [body(): query = lax.all_gather(query_own, KV, axis=2, tiled=True)]
  transfers between devices with their start and end apart: 4 -> 0, of which waited for: 3 -> 0; matrix products, arithmetic and copies ran while one was open for 9% -> 0% of each run, Pallas kernels for 0% -> 0%
where the time goes in v1:
time: 58.3 us; the launch traced here: 57.3 us
  Pallas kernels  52.9 us (91%)
  local copies, waits for them, and re-layouts  3.72 us (6%)
  between operations  0.64 us (1%)
    pallas_call x1, Pallas kernels, body(): pl.pallas_call(functools.partial(kernel, scale), out_shape=(jax.ShapeDtyp...  52.9 us
    unnamed x2, local copies, waits for them, and re-layouts  2.53 us
    slice x1, local copies, waits for them, and re-layouts, body(): return (attended.reshape(seqs, drafts, heads, -1), accepted, total[0, 0])  1.19 us

profile of v1, /device:TPU:0, one launch (start us, length us, event | category | flops | bytes accessed | tf_op | source)
XLA Modules:
  0.0 57.3 jit_solution(18142508038793724151)
XLA Ops:
  0.6 52.9 %verify.1 = (bf16[128,128]{1,0:T(8,128)(2,1)}, s32[4]{0:T(128)}, s32[8,128]{1,0:T(8,128)}) custom-call(bf16[128,128]{1,0:T(8,128)(2,1)} %bitcast.6, bf16[128,64]{1,0:T(8,128)(2,1)} %bitcast.7, bf16[4,128,512]{2,1,0:T(8,128)(2,1)} %wuk_hbm.1, bf16[4,512,128]{2,1,0:T(8,128)(2,1)} %wuv_hbm.1, bf16[64,64,576]{2,1,0:T(8,128)(2,1)} %cache_hbm.1, ...), custom_call_target="tpu_custom_call" | custom-call | tf_op jit(solution)/shard_map/verify/pallas_call | solution.py:392
  53.6 1.2 %slice.3 = s32[1,1]{1,0:T(1,128)} slice(s32[8,128]{1,0:T(8,128)} %get-tuple-element.8), slice={[0:1], [0:1]} | slice | bytes 8 | tf_op jit(solution)/shard_map/slice | solution.py:417
  54.8 1.4 %copy.14 = bf16[4,8,4,128]{3,2,1,0:T(4,128)(2,1)} copy(bf16[4,8,4,128]{3,2,1,0:T(4,128)(2,1)} %bitcast.8) | data formatting | bytes 65536
  56.1 1.1 %copy.15 = s32[4]{0:T(128)} copy(s32[4]{0:T(128)} %get-tuple-element.13) | data formatting | bytes 32

commit v2 on v1

v2 whole, which is shorter than its diff:
```python
import functools
import math

import jax
import jax.numpy as jnp
from jax import lax
from jax.experimental import pallas as pl
from jax.experimental.pallas import tpu as pltpu
from jax.sharding import Mesh
from jax.sharding import PartitionSpec as P

KV = ("kv_0", "kv_1", "kv_2")
SEQ_KV = ("seq", "kv_0", "kv_1", "kv_2")
AXES = (("kv_1", "kv_0"), ("kv_0", "kv_1"))
POS = (0, 1, 3, 2)
GROUPS = ((0, 1), (1, 2), (3, 1))
RING = 4
PAIRS = ((0, 0), (0, 1), (1, 0), (1, 1))
MASKED = -1e30
MESH = pl.DeviceIdType.MESH
NT = (((1,), (1,)), ((), ()))
NN = (((1,), (0,)), ((), ()))


def dot(a, b, dims=NN):
    return lax.dot_general(a, b, dims, preferred_element_type=jnp.float32)


def shifted(axis, by):
    return {axis: lax.rem(lax.axis_index(axis) + by, RING)}


def kernel(
    scale,
    qn_hbm, qr_hbm, wuk_hbm, wuv_hbm, cache_hbm, draft_hbm, pt_ref, len_ref, flags_ref,
    out_ref, acc_ref, tot_ref,
    qn, qr, wuk, wuv, pool, draft, kbuf, qbuf, nsend, nrecv, ssend, srecv,
    csend, crecv, tsend, trecv, nd, md, ld, lo, count, counts,
    in_sem, key_s, key_r, q1_s, q1_r, q2_s, q2_r, n_s, n_r, s_s, s_r, c_s, c_r, t_s, t_r,
    a_s, a_r, far_sem,
):
    rate = scale * math.log2(math.e)
    rows = qbuf.shape[3]
    latent = nsend.shape[5]
    seqs, ctx = kbuf.shape[0], kbuf.shape[1]
    own_ctx = ctx // 2
    pages, page = pt_ref.shape[2], pool.shape[1]
    heads = wuk.shape[0]
    line = RING * rows
    core = lax.axis_index("kv_2")
    chip = lax.axis_index("kv_0") * RING + lax.axis_index("kv_1")
    partner = {"kv_2": 1 - core}

    small = []
    for i, (src, dst) in enumerate(
        ((qn_hbm, qn), (wuk_hbm, wuk), (qr_hbm, qr), (draft_hbm, draft), (wuv_hbm, wuv))
    ):
        small.append(pltpu.make_async_copy(src, dst, in_sem.at[i]))
    for copy in small[:4]:
        copy.start()
    quarter = pool.shape[0] // 4
    pools = []
    for i in range(4):
        part = pl.ds(i * quarter, quarter)
        pools.append(pltpu.make_async_copy(cache_hbm.at[part], pool.at[part], in_sem.at[5 + i]))
        pools[-1].start()
    small[4].start()

    barrier = pltpu.get_barrier_semaphore()
    near = [shifted(axis, by) for axis in ("kv_0", "kv_1", "seq") for by in (1, 3)]
    peers = [partner] + near
    for peer in peers:
        pl.semaphore_signal(barrier, inc=1, device_id=peer, device_id_type=MESH)

    def remote(src, dst, send, recv, peer):
        return pltpu.make_async_remote_copy(
            src_ref=src, dst_ref=dst, send_sem=send, recv_sem=recv,
            device_id=peer, device_id_type=MESH,
        )

    mine = jnp.int32(0)
    for s in range(seqs):
        run, total = jnp.int32(1), jnp.int32(0)
        for i in range(flags_ref.shape[1]):
            run = run * flags_ref[s, i]
            total = total + run
        acc_ref[s] = total
        mine = mine + total
    count[...] = jnp.full(count.shape, mine, jnp.int32)

    def arrived(dst, recv):
        remote(dst, dst, in_sem.at[0], recv, partner).wait_recv()

    for copy in small[:4]:
        copy.wait()
    row = lax.broadcasted_iota(jnp.int32, qn.shape, 0)
    qn_f = qn[...].astype(jnp.float32)
    q_lat = jnp.zeros((qn.shape[0], latent), jnp.float32)
    for h in range(heads):
        part = jnp.where(lax.rem(row, heads) == h, qn_f, 0.0).astype(jnp.bfloat16)
        q_lat = q_lat + dot(part, wuk[h])
    q_lat = q_lat.astype(jnp.bfloat16)
    for s in range(seqs):
        h, u = s // 2, s % 2
        qbuf[h, 0, 0, :, u * latent:(u + 1) * latent] = q_lat[s * rows:(s + 1) * rows]
    for h in range(2):
        ropes = [qr[(2 * h + u) * rows:(2 * h + u + 1) * rows] for u in range(2)]
        qbuf[h, 0, 0, :, 2 * latent:] = jnp.concatenate(ropes, axis=1)

    pl.semaphore_wait(barrier, len(peers))
    for peer in near:
        pl.semaphore_signal(far_sem, inc=1, device_id=peer, device_id_type=MESH)

    started = []

    def send(copy):
        copy.start()
        started.append(copy)

    def stage_one(h, by):
        i = by // 2
        send(remote(
            qbuf.at[h, 0, 0], qbuf.at[h, 0, RING - by], q1_s.at[h, i], q1_r.at[h, i],
            shifted(AXES[h][0], by),
        ))

    def stage_one_far(h, by):
        i = by // 2
        half = pl.ds(i * (rows // 2), rows // 2)
        send(remote(
            qbuf.at[h, 0, RING - by, half], qbuf.at[h, 0, 2, half], q1_s.at[h, 2 + i],
            q1_r.at[h, 2 + i], shifted(AXES[h][0], by),
        ))

    def stage_two(h, j, by):
        i = by // 2
        send(remote(
            qbuf.at[h, 0, j], qbuf.at[h, POS[RING - by], j], q2_s.at[h, i, j],
            q2_r.at[h, i, j], shifted(AXES[h][1], by),
        ))

    def stage_two_far(h, j, by):
        send(remote(
            qbuf.at[h, POS[RING - by], j], qbuf.at[h, POS[2], j], q2_s.at[h, 2, j],
            q2_r.at[h, 2, j], shifted(AXES[h][1], by),
        ))

    for h in range(2):
        for by in (1, 3):
            stage_one(h, by)
    for h in range(2):
        for by in (1, 3):
            stage_two(h, 0, by)

    for copy in pools:
        copy.wait()
    key_copies = []

    def send_keys(s):
        part = pl.ds(core * own_ctx, own_ctx)
        copy = remote(kbuf.at[s, part], kbuf.at[s, part], key_s.at[s], key_r.at[s], partner)
        copy.start()
        key_copies.append(copy)

    for s in range(seqs):
        def place(t, _, s=s):
            tokens = pool[pt_ref[s, 0, t]]
            at = pl.ds(pl.multiple_of(core * own_ctx + t * page, page), page)
            kbuf[s, at, :latent] = tokens[:, :latent]
            rope = tokens[:, latent:]
            none = jnp.zeros_like(rope)
            both = [rope, none] if s % 2 == 0 else [none, rope]
            kbuf[s, at, latent:] = jnp.concatenate(both, axis=1)
            return 0

        lax.fori_loop(0, pages, place, 0)
        if s:
            send_keys(s - 1)

    for h in range(2):
        for by in (1, 3):
            arrived(qbuf.at[h, 0, RING - by], q1_r.at[h, by // 2])
            stage_one_far(h, by)
    for h in range(2):
        for by in (1, 3):
            stage_two(h, by, by)
    for h in range(2):
        for by in (1, 3):
            stage_two(h, RING - by, by)
    send_keys(seqs - 1)

    keys_d = draft[:, :latent]
    d_score = dot(q_lat, keys_d, NT) + dot(qr[...], draft[:, latent:], NT)
    per_seq, drafts = qn.shape[0] // seqs, draft.shape[0] // seqs
    r = lax.broadcasted_iota(jnp.int32, d_score.shape, 0)
    c = lax.broadcasted_iota(jnp.int32, d_score.shape, 1)
    seen = (r // per_seq == c // drafts) & (lax.rem(c, drafts) <= lax.rem(r, per_seq) // heads)
    d_score = jnp.where(seen, d_score, MASKED)
    d_top = jnp.max(d_score, axis=1, keepdims=True)
    d_w = jnp.where(seen, jnp.exp2((d_score - d_top) * rate), 0.0)
    md[...] = jnp.broadcast_to(d_top, md.shape)
    ld[...] = jnp.broadcast_to(jnp.sum(d_w, axis=1, keepdims=True), ld.shape)
    nd[...] = dot(d_w.astype(jnp.bfloat16), keys_d)

    for h in range(2):
        for i in range(2):
            half = pl.ds(i * (rows // 2), rows // 2)
            arrived(qbuf.at[h, 0, 2, half], q1_r.at[h, 2 + i])
        for by in (1, 3):
            stage_two(h, 2, by)

    pl.semaphore_wait(far_sem, len(near))
    tallies = []
    for by in range(1, RING):
        copy = remote(
            count, counts.at[RING - by - 1], a_s.at[by - 1], a_r.at[RING - by - 1],
            shifted("seq", by),
        )
        copy.start()
        tallies.append(copy)

    def relay(i):
        for h in range(2):
            for by, js in ((1, (0, 1)), (3, (3, 2))):
                arrived(qbuf.at[h, POS[RING - by], js[i]], q2_r.at[h, by // 2, js[i]])
                stage_two_far(h, js[i], by)

    heavy = []

    def compute(h, group):
        first, places = group
        height = places * line
        for place in range(first, first + places):
            slot = POS[place]
            left = {0: (), 1: (0, 1), 2: (0, 1, 2, 3), 3: (2, 3)}[slot]
            for j in left:
                arrived(qbuf.at[h, place, j], q2_r.at[h, {1: 1, 2: 2, 3: 0}[slot], j])

        def one(u):
            s = 2 * h + u
            at = slice(u * latent, (u + 1) * latent)
            q = qbuf[h, first:first + places, :, :, at].reshape(height, latent)
            qrope = qbuf[h, first:first + places, :, :, 2 * latent:].reshape(height, 128)
            score = dot(q, kbuf[s, :, :latent], NT) + dot(qrope, kbuf[s, :, latent:], NT)
            position = chip * ctx + lax.broadcasted_iota(jnp.int32, (1, ctx), 1)
            valid = position < len_ref[s]
            score = jnp.where(valid, score, MASKED)
            top = jnp.max(score, axis=1, keepdims=True)
            weight = jnp.where(valid, jnp.exp2((score - top) * rate), 0.0)
            total = jnp.sum(weight, axis=1, keepdims=True)
            lane = lax.broadcasted_iota(jnp.int32, (height, 128), 1)
            stats = jnp.transpose(jnp.where(lane == 0, top, total))[:8]
            for k in range(places):
                ssend[h, first + k, u] = stats[:, k * line:(k + 1) * line]
            numer = dot(weight.astype(jnp.bfloat16), kbuf[s, :, :latent])
            numer = numer.astype(jnp.bfloat16).reshape(places, RING, rows, latent)
            nsend[h, first:first + places, u] = numer

        one(0)
        one(1)
        for u in range(2):
            for place in range(first, first + places):
                slot = POS[place]
                if slot:
                    back, peer = RING - slot - 1, shifted(AXES[h][1], slot)
                    copies = (
                        remote(
                            ssend.at[h, place, u], srecv.at[h, back, u], s_s.at[h, slot - 1, u],
                            s_r.at[h, back, u], peer,
                        ),
                        remote(
                            nsend.at[h, place, u], nrecv.at[h, back, u], n_s.at[h, slot - 1, u],
                            n_r.at[h, back, u], peer,
                        ),
                    )
                    for copy in copies:
                        copy.start()
                        heavy.append(copy)

    other = pl.ds((1 - core) * own_ctx, own_ctx)
    for g, group in enumerate(GROUPS):
        for h in range(2):
            if g == 0:
                for s in (2 * h, 2 * h + 1):
                    arrived(kbuf.at[s, other], key_r.at[s])
            compute(h, group)
            if g == 0:
                relay(h)

    light = []
    for h, u in PAIRS:
        for slot in (1, 3, 2):
            arrived(srecv.at[h, slot - 1, u], s_r.at[h, slot - 1, u])
            arrived(nrecv.at[h, slot - 1, u], n_r.at[h, slot - 1, u])
        stat = [ssend[h, 0, u]] + [srecv[h, k, u] for k in range(RING - 1)]
        tops = [x[0:1] for x in stat]
        top = functools.reduce(jnp.maximum, tops)
        ws = [jnp.exp2((x - top) * rate) for x in tops]
        total = sum(w * x[1:2] for w, x in zip(ws, stat))
        sub = lax.broadcasted_iota(jnp.int32, (8, line), 0)
        tsend[h, u] = jnp.where(sub == 0, top, total)
        pick = ws[3]
        for k in (2, 1, 0):
            pick = jnp.where(sub == k, ws[k], pick)
        cols = jnp.transpose(pick)
        mixed = jnp.zeros((line, latent), jnp.float32)
        for k in range(RING):
            part = nsend[h, 0, u] if k == 0 else nrecv[h, k - 1, u]
            part = part.reshape(line, latent).astype(jnp.float32)
            mixed = mixed + cols[:, k:k + 1] * part
        csend[h, u] = mixed.astype(jnp.bfloat16).reshape(RING, rows, latent)
        for j in (2, 1, 3):
            back, peer = RING - j - 1, shifted(AXES[h][0], j)
            copies = (
                remote(
                    tsend.at[h, u], trecv.at[h, back, u], t_s.at[h, j - 1, u],
                    t_r.at[h, back, u], peer,
                ),
                remote(
                    csend.at[h, u, j], crecv.at[h, back, u], c_s.at[h, j - 1, u],
                    c_r.at[h, back, u], peer,
                ),
            )
            for copy in copies:
                copy.start()
                light.append(copy)

    for h, u in PAIRS:
        for slot in range(1, RING):
            arrived(trecv.at[h, slot - 1, u], t_r.at[h, slot - 1, u])
            arrived(crecv.at[h, slot - 1, u], c_r.at[h, slot - 1, u])
        here = pl.ds((2 * h + u) * rows, rows)
        tops, totals, parts = [md[here, 0:1]], [ld[here, 0:1]], [nd[here]]
        for slot in range(RING):
            j = (RING - slot) % RING
            stat = tsend[h, u] if slot == 0 else trecv[h, slot - 1, u]
            cols = jnp.transpose(stat)[j * rows:(j + 1) * rows]
            tops.append(cols[:, 0:1])
            totals.append(cols[:, 1:2])
            part = csend[h, u, 0] if slot == 0 else crecv[h, slot - 1, u]
            parts.append(part.astype(jnp.float32))
        top = functools.reduce(jnp.maximum, tops)
        ws = [jnp.exp2((x - top) * rate) for x in tops]
        total = sum(w * x for w, x in zip(ws, totals))
        mixed = sum(w * x for w, x in zip(ws, parts))
        lo[here] = (mixed / total).astype(jnp.bfloat16)

    small[4].wait()
    latent_out = lo[...]
    attended = jnp.zeros(out_ref.shape, jnp.float32)
    row = lax.broadcasted_iota(jnp.int32, out_ref.shape, 0)
    for h in range(heads):
        attended = jnp.where(lax.rem(row, heads) == h, dot(latent_out, wuv[h]), attended)
    out_ref[...] = attended.astype(out_ref.dtype)

    for copy in tallies:
        copy.wait_recv()
    tot_ref[...] = count[...] + counts[0] + counts[1] + counts[2]
    for copy in tallies + started + key_copies + heavy + light:
        copy.wait_send()


def hand_over(a_ref, n_ref, t_ref, a_out, n_out, t_out):
    a_out[...] = a_ref[...]
    for s in range(n_ref.shape[0]):
        n_out[s] = n_ref[s]
    t_out[0] = jnp.max(t_ref[...])


def body(q_nope, q_rope, w_uk, w_uv, cache, page_table, lengths, draft_kv, flags):
    seqs, drafts, heads, nope = q_nope.shape
    latent, width = w_uk.shape[2], cache.shape[2]
    rope = width - latent
    scale = (nope + rope) ** -0.5
    count = seqs * drafts * heads
    rows = drafts * heads
    ctx = 2 * page_table.shape[2] * cache.shape[1]
    bf16, f32 = jnp.bfloat16, jnp.float32
    hbm = pl.BlockSpec(memory_space=pl.ANY)
    smem = pl.BlockSpec(memory_space=pltpu.SMEM)
    vmem = pl.BlockSpec(memory_space=pltpu.VMEM)
    dma = pltpu.SemaphoreType.DMA
    scratch = [
        pltpu.VMEM((count, nope), bf16),
        pltpu.VMEM((count, rope), bf16),
        pltpu.VMEM(w_uk.shape, bf16),
        pltpu.VMEM(w_uv.shape, bf16),
        pltpu.VMEM(cache.shape, bf16),
        pltpu.VMEM((seqs * drafts, width), bf16),
        pltpu.VMEM((seqs, ctx, latent + 2 * rope), bf16),
        pltpu.VMEM((2, RING, RING, rows, 2 * (latent + rope)), bf16),
        pltpu.VMEM((2, RING, 2, RING, rows, latent), bf16),
        pltpu.VMEM((2, RING - 1, 2, RING, rows, latent), bf16),
        pltpu.VMEM((2, RING, 2, 8, RING * rows), f32),
        pltpu.VMEM((2, RING - 1, 2, 8, RING * rows), f32),
        pltpu.VMEM((2, 2, RING, rows, latent), bf16),
        pltpu.VMEM((2, RING - 1, 2, rows, latent), bf16),
        pltpu.VMEM((2, 2, 8, RING * rows), f32),
        pltpu.VMEM((2, RING - 1, 2, 8, RING * rows), f32),
        pltpu.VMEM((count, latent), f32),
        pltpu.VMEM((count, 128), f32),
        pltpu.VMEM((count, 128), f32),
        pltpu.VMEM((count, latent), bf16),
        pltpu.VMEM((8, 128), jnp.int32),
        pltpu.VMEM((RING - 1, 8, 128), jnp.int32),
        dma((9,)),
        dma((seqs,)), dma((seqs,)),
        dma((2, 4)), dma((2, 4)),
        dma((2, RING - 1, RING)), dma((2, RING - 1, RING)),
        dma((2, RING - 1, 2)), dma((2, RING - 1, 2)),
        dma((2, RING - 1, 2)), dma((2, RING - 1, 2)),
        dma((2, RING - 1, 2)), dma((2, RING - 1, 2)),
        dma((2, RING - 1, 2)), dma((2, RING - 1, 2)),
        dma((RING - 1,)), dma((RING - 1,)),
        pltpu.SemaphoreType.REGULAR,
    ]
    attended, accepted, total = pl.pallas_call(
        functools.partial(kernel, scale),
        out_shape=(
            jax.ShapeDtypeStruct((count, w_uv.shape[2]), bf16),
            jax.ShapeDtypeStruct((seqs,), jnp.int32),
            jax.ShapeDtypeStruct((8, 128), jnp.int32),
        ),
        in_specs=[hbm] * 6 + [smem] * 3,
        out_specs=(vmem, smem, vmem),
        scratch_shapes=scratch,
        compiler_params=pltpu.CompilerParams(
            collective_id=0, has_side_effects=True, vmem_limit_bytes=60 * 1024 * 1024
        ),
        name="verify",
    )(
        q_nope.reshape(count, nope),
        q_rope.reshape(count, rope),
        w_uk,
        w_uv,
        cache,
        draft_kv.reshape(seqs * drafts, width),
        page_table,
        lengths,
        flags,
    )
    attended, accepted, total = pl.pallas_call(
        hand_over,
        out_shape=(
            jax.ShapeDtypeStruct(attended.shape, bf16),
            jax.ShapeDtypeStruct((seqs,), jnp.int32),
            jax.ShapeDtypeStruct((1,), jnp.int32),
        ),
        in_specs=[vmem, smem, vmem],
        out_specs=(vmem, smem, smem),
        name="hand_over",
    )(attended, accepted, total)
    return attended.reshape(seqs, drafts, heads, -1), accepted, total.reshape(())


def solution(mesh):
    split = Mesh(mesh.devices.reshape(mesh.shape["seq"], RING, RING, 2), SEQ_KV)
    return jax.shard_map(
        body,
        mesh=split,
        in_specs=(
            P("seq", None, KV, None),
            P("seq", None, KV, None),
            P(KV, None, None),
            P(KV, None, None),
            P(SEQ_KV, None, None),
            P("seq", KV, None),
            P("seq"),
            P("seq", None, None),
            P("seq", None),
        ),
        out_specs=(P("seq", None, KV, None), P("seq"), P()),
        check_vma=False,
    )
```

time: 58.3 us -> 53.3 us (0.914); the launches traced: 57.3 us -> 53.1 us
  local copies, waits for them, and re-layouts: 3.72 us -> 0 us
  Pallas kernels: 52.9 us -> 52.3 us
    unnamed x2 -> x0, local copies, waits for them, and re-layouts: 2.53 us -> none
    pallas_call x1, Pallas kernels: 52.9 us -> 50.8 us  [body(): pl.pallas_call(functools.partial(kernel, scale), out_shape=(jax.ShapeDtyp...]
    pallas_call x0 -> x1, Pallas kernels: none -> 1.51 us  [body(): pl.pallas_call(hand_over, out_shape=(jax.ShapeDtypeStruct(attended.shape,...]
    slice x1 -> x0, local copies, waits for them, and re-layouts: 1.19 us -> none  [body(): return (attended.reshape(seqs, drafts, heads, -1), accepted, total[0, 0])]
where the time goes in v2:
time: 53.3 us; the launch traced here: 53.1 us
  Pallas kernels  52.3 us (98%)
  between operations  0.8 us (2%)
    pallas_call x1, Pallas kernels, body(): pl.pallas_call(functools.partial(kernel, scale), out_shape=(jax.ShapeDtyp...  50.8 us
    pallas_call x1, Pallas kernels, body(): pl.pallas_call(hand_over, out_shape=(jax.ShapeDtypeStruct(attended.shape,...  1.51 us

profile of v2, /device:TPU:0, one launch (start us, length us, event | category | flops | bytes accessed | tf_op | source)
XLA Modules:
  0.0 53.1 jit_solution(8988933245500938785)
XLA Ops:
  0.6 50.8 %verify.1 = (bf16[128,128]{1,0:T(8,128)(2,1)}, s32[4]{0:T(128)}, s32[8,128]{1,0:T(8,128)}) custom-call(bf16[128,128]{1,0:T(8,128)(2,1)} %bitcast.6, bf16[128,64]{1,0:T(8,128)(2,1)} %bitcast.7, bf16[4,128,512]{2,1,0:T(8,128)(2,1)} %wuk_hbm.1, bf16[4,512,128]{2,1,0:T(8,128)(2,1)} %wuv_hbm.1, bf16[64,64,576]{2,1,0:T(8,128)(2,1)} %cache_hbm.1, ...), custom_call_target="tpu_custom_call" | custom-call | tf_op jit(solution)/shard_map/verify/pallas_call | solution.py:417
  51.4 1.5 %hand_over.1 = (bf16[128,128]{1,0:T(8,128)(2,1)}, s32[4]{0:T(128)}, s32[1]{0:T(128)}) custom-call(bf16[128,128]{1,0:T(8,128)(2,1)} %get-tuple-element.9.a_ref, s32[4]{0:T(128)} %get-tuple-element.10.n_ref, s32[8,128]{1,0:T(8,128)} %get-tuple-element.11.t_ref), custom_call_target="tpu_custom_call" | custom-call | tf_op jit(solution)/shard_map/hand_over/pallas_call | solution.py:442

commit v3 on v2

--- a/solution.py
+++ b/solution.py
@@ -12,10 +12,12 @@
 KV = ("kv_0", "kv_1", "kv_2")
 SEQ_KV = ("seq", "kv_0", "kv_1", "kv_2")
 AXES = (("kv_1", "kv_0"), ("kv_0", "kv_1"))
-POS = (0, 1, 3, 2)
-GROUPS = ((0, 1), (1, 2), (3, 1))
+PLACE = (3, 0, 2, 1)
+SLOT = (1, 3, 2, 0)
+HOME = PLACE[0]
+GROUPS = ((0, 2), (2, 2))
 RING = 4
-PAIRS = ((0, 0), (0, 1), (1, 0), (1, 1))
+PAIRS = ((0, 0), (1, 0), (0, 1), (1, 1))
 MASKED = -1e30
 MESH = pl.DeviceIdType.MESH
 NT = (((1,), (1,)), ((), ()))
@@ -102,10 +104,10 @@
     q_lat = q_lat.astype(jnp.bfloat16)
     for s in range(seqs):
         h, u = s // 2, s % 2
-        qbuf[h, 0, 0, :, u * latent:(u + 1) * latent] = q_lat[s * rows:(s + 1) * rows]
+        qbuf[h, HOME, 0, :, u * latent:(u + 1) * latent] = q_lat[s * rows:(s + 1) * rows]
     for h in range(2):
         ropes = [qr[(2 * h + u) * rows:(2 * h + u + 1) * rows] for u in range(2)]
-        qbuf[h, 0, 0, :, 2 * latent:] = jnp.concatenate(ropes, axis=1)
+        qbuf[h, HOME, 0, :, 2 * latent:] = jnp.concatenate(ropes, axis=1)
 
     pl.semaphore_wait(barrier, len(peers))
     for peer in near:
@@ -120,7 +122,7 @@
     def stage_one(h, by):
         i = by // 2
         send(remote(
-            qbuf.at[h, 0, 0], qbuf.at[h, 0, RING - by], q1_s.at[h, i], q1_r.at[h, i],
+            qbuf.at[h, HOME, 0], qbuf.at[h, HOME, RING - by], q1_s.at[h, i], q1_r.at[h, i],
             shifted(AXES[h][0], by),
         ))
 
@@ -128,20 +130,20 @@
         i = by // 2
         half = pl.ds(i * (rows // 2), rows // 2)
         send(remote(
-            qbuf.at[h, 0, RING - by, half], qbuf.at[h, 0, 2, half], q1_s.at[h, 2 + i],
+            qbuf.at[h, HOME, RING - by, half], qbuf.at[h, HOME, 2, half], q1_s.at[h, 2 + i],
             q1_r.at[h, 2 + i], shifted(AXES[h][0], by),
         ))
 
     def stage_two(h, j, by):
         i = by // 2
         send(remote(
-            qbuf.at[h, 0, j], qbuf.at[h, POS[RING - by], j], q2_s.at[h, i, j],
+            qbuf.at[h, HOME, j], qbuf.at[h, PLACE[RING - by], j], q2_s.at[h, i, j],
             q2_r.at[h, i, j], shifted(AXES[h][1], by),
         ))
 
     def stage_two_far(h, j, by):
         send(remote(
-            qbuf.at[h, POS[RING - by], j], qbuf.at[h, POS[2], j], q2_s.at[h, 2, j],
+            qbuf.at[h, PLACE[RING - by], j], qbuf.at[h, PLACE[2], j], q2_s.at[h, 2, j],
             q2_r.at[h, 2, j], shifted(AXES[h][1], by),
         ))
 
@@ -179,7 +181,7 @@
 
     for h in range(2):
         for by in (1, 3):
-            arrived(qbuf.at[h, 0, RING - by], q1_r.at[h, by // 2])
+            arrived(qbuf.at[h, HOME, RING - by], q1_r.at[h, by // 2])
             stage_one_far(h, by)
     for h in range(2):
         for by in (1, 3):
@@ -205,7 +207,7 @@
     for h in range(2):
         for i in range(2):
             half = pl.ds(i * (rows // 2), rows // 2)
-            arrived(qbuf.at[h, 0, 2, half], q1_r.at[h, 2 + i])
+            arrived(qbuf.at[h, HOME, 2, half], q1_r.at[h, 2 + i])
         for by in (1, 3):
             stage_two(h, 2, by)
 
@@ -222,77 +224,82 @@
     def relay(i):
         for h in range(2):
             for by, js in ((1, (0, 1)), (3, (3, 2))):
-                arrived(qbuf.at[h, POS[RING - by], js[i]], q2_r.at[h, by // 2, js[i]])
+                arrived(qbuf.at[h, PLACE[RING - by], js[i]], q2_r.at[h, by // 2, js[i]])
                 stage_two_far(h, js[i], by)
 
     heavy = []
 
-    def compute(h, group):
+    def arrive_all(h, group):
         first, places = group
-        height = places * line
         for place in range(first, first + places):
-            slot = POS[place]
+            slot = SLOT[place]
             left = {0: (), 1: (0, 1), 2: (0, 1, 2, 3), 3: (2, 3)}[slot]
             for j in left:
                 arrived(qbuf.at[h, place, j], q2_r.at[h, {1: 1, 2: 2, 3: 0}[slot], j])
 
-        def one(u):
-            s = 2 * h + u
-            at = slice(u * latent, (u + 1) * latent)
-            q = qbuf[h, first:first + places, :, :, at].reshape(height, latent)
-            qrope = qbuf[h, first:first + places, :, :, 2 * latent:].reshape(height, 128)
-            score = dot(q, kbuf[s, :, :latent], NT) + dot(qrope, kbuf[s, :, latent:], NT)
-            position = chip * ctx + lax.broadcasted_iota(jnp.int32, (1, ctx), 1)
-            valid = position < len_ref[s]
-            score = jnp.where(valid, score, MASKED)
-            top = jnp.max(score, axis=1, keepdims=True)
-            weight = jnp.where(valid, jnp.exp2((score - top) * rate), 0.0)
-            total = jnp.sum(weight, axis=1, keepdims=True)
-            lane = lax.broadcasted_iota(jnp.int32, (height, 128), 1)
-            stats = jnp.transpose(jnp.where(lane == 0, top, total))[:8]
-            for k in range(places):
-                ssend[h, first + k, u] = stats[:, k * line:(k + 1) * line]
-            numer = dot(weight.astype(jnp.bfloat16), kbuf[s, :, :latent])
-            numer = numer.astype(jnp.bfloat16).reshape(places, RING, rows, latent)
-            nsend[h, first:first + places, u] = numer
-
-        one(0)
-        one(1)
-        for u in range(2):
-            for place in range(first, first + places):
-                slot = POS[place]
-                if slot:
-                    back, peer = RING - slot - 1, shifted(AXES[h][1], slot)
-                    copies = (
-                        remote(
-                            ssend.at[h, place, u], srecv.at[h, back, u], s_s.at[h, slot - 1, u],
-                            s_r.at[h, back, u], peer,
-                        ),
-                        remote(
-                            nsend.at[h, place, u], nrecv.at[h, back, u], n_s.at[h, slot - 1, u],
-                            n_r.at[h, back, u], peer,
-                        ),
-                    )
-                    for copy in copies:
-                        copy.start()
-                        heavy.append(copy)
-
+    def attend(h, u, group):
+        first, places = group
+        height = places * line
+        s = 2 * h + u
+        at = slice(u * latent, (u + 1) * latent)
+        q = qbuf[h, first:first + places, :, :, at].reshape(height, latent)
+        qrope = qbuf[h, first:first + places, :, :, 2 * latent:].reshape(height, 128)
+        score = dot(q, kbuf[s, :, :latent], NT) + dot(qrope, kbuf[s, :, latent:], NT)
+        position = chip * ctx + lax.broadcasted_iota(jnp.int32, (1, ctx), 1)
+        valid = position < len_ref[s]
+        score = jnp.where(valid, score, MASKED)
+        top = jnp.max(score, axis=1, keepdims=True)
+        weight = jnp.where(valid, jnp.exp2((score - top) * rate), 0.0)
+        total = jnp.sum(weight, axis=1, keepdims=True)
+        lane = lax.broadcasted_iota(jnp.int32, (height, 128), 1)
+        stats = jnp.transpose(jnp.where(lane == 0, top, total))[:8]
+        for k in range(places):
+            ssend[h, first + k, u] = stats[:, k * line:(k + 1) * line]
+        numer = dot(weight.astype(jnp.bfloat16), kbuf[s, :, :latent])
+        nsend[h, first:first + places, u] = numer.astype(jnp.bfloat16).reshape(
+            places, RING, rows, latent
+        )
+
+    def send_sums(h, u, place):
+        slot = SLOT[place]
+        back, peer = RING - slot - 1, shifted(AXES[h][1], slot)
+        copies = (
+            remote(
+                ssend.at[h, place, u], srecv.at[h, back, u], s_s.at[h, slot - 1, u],
+                s_r.at[h, back, u], peer,
+            ),
+            remote(
+                nsend.at[h, place, u], nrecv.at[h, back, u], n_s.at[h, slot - 1, u],
+                n_r.at[h, back, u], peer,
+            ),
+        )
+        for copy in copies:
+            copy.start()
+            heavy.append(copy)
+
+    relay(0)
+    relay(1)
     other = pl.ds((1 - core) * own_ctx, own_ctx)
     for g, group in enumerate(GROUPS):
         for h in range(2):
-            if g == 0:
-                for s in (2 * h, 2 * h + 1):
-                    arrived(kbuf.at[s, other], key_r.at[s])
-            compute(h, group)
-            if g == 0:
-                relay(h)
+            arrive_all(h, group)
+        for u in range(2):
+            for h in range(2):
+                if g == 0:
+                    arrived(kbuf.at[2 * h + u, other], key_r.at[2 * h + u])
+            for h in range(2):
+                attend(h, u, group)
+            for h in range(2):
+                for place in range(group[0], group[0] + group[1]):
+                    if place != HOME:
+                        send_sums(h, u, place)
 
     light = []
     for h, u in PAIRS:
         for slot in (1, 3, 2):
             arrived(srecv.at[h, slot - 1, u], s_r.at[h, slot - 1, u])
             arrived(nrecv.at[h, slot - 1, u], n_r.at[h, slot - 1, u])
-        stat = [ssend[h, 0, u]] + [srecv[h, k, u] for k in range(RING - 1)]
+        stat = [ssend[h, HOME, u]] + [srecv[h, k, u] for k in range(RING - 1)]
         tops = [x[0:1] for x in stat]
         top = functools.reduce(jnp.maximum, tops)
         ws = [jnp.exp2((x - top) * rate) for x in tops]
@@ -305,7 +312,7 @@
         cols = jnp.transpose(pick)
         mixed = jnp.zeros((line, latent), jnp.float32)
         for k in range(RING):
-            part = nsend[h, 0, u] if k == 0 else nrecv[h, k - 1, u]
+            part = nsend[h, HOME, u] if k == 0 else nrecv[h, k - 1, u]
             part = part.reshape(line, latent).astype(jnp.float32)
             mixed = mixed + cols[:, k:k + 1] * part
         csend[h, u] = mixed.astype(jnp.bfloat16).reshape(RING, rows, latent)

time: 53.3 us -> 49.4 us (0.927)
  Pallas kernels: 52.3 us -> 48.5 us
    pallas_call x1, Pallas kernels: 50.8 us -> 47 us  [body(): pl.pallas_call(functools.partial(kernel, scale), out_shape=(jax.ShapeDtyp...]
where the time goes in v3:
time: 49.4 us; the launch traced here: 49.2 us
  Pallas kernels  48.5 us (98%)
  between operations  0.64 us (1%)
    pallas_call x1, Pallas kernels, body(): pl.pallas_call(functools.partial(kernel, scale), out_shape=(jax.ShapeDtyp...  47 us
    pallas_call x1, Pallas kernels, body(): pl.pallas_call(hand_over, out_shape=(jax.ShapeDtypeStruct(attended.shape,...  1.51 us

profile of v3, /device:TPU:0, one launch (start us, length us, event | category | flops | bytes accessed | tf_op | source)
XLA Modules:
  0.0 49.2 jit_solution(3308374403181010906)
XLA Ops:
  0.6 47.0 %verify.1 = (bf16[128,128]{1,0:T(8,128)(2,1)}, s32[4]{0:T(128)}, s32[8,128]{1,0:T(8,128)}) custom-call(bf16[128,128]{1,0:T(8,128)(2,1)} %bitcast.6, bf16[128,64]{1,0:T(8,128)(2,1)} %bitcast.7, bf16[4,128,512]{2,1,0:T(8,128)(2,1)} %wuk_hbm.1, bf16[4,512,128]{2,1,0:T(8,128)(2,1)} %wuv_hbm.1, bf16[64,64,576]{2,1,0:T(8,128)(2,1)} %cache_hbm.1, ...), custom_call_target="tpu_custom_call" | custom-call | tf_op jit(solution)/shard_map/verify/pallas_call | solution.py:424
  47.7 1.5 %hand_over.1 = (bf16[128,128]{1,0:T(8,128)(2,1)}, s32[4]{0:T(128)}, s32[1]{0:T(128)}) custom-call(bf16[128,128]{1,0:T(8,128)(2,1)} %get-tuple-element.9.a_ref, s32[4]{0:T(128)} %get-tuple-element.10.n_ref, s32[8,128]{1,0:T(8,128)} %get-tuple-element.11.t_ref), custom_call_target="tpu_custom_call" | custom-call | tf_op jit(solution)/shard_map/hand_over/pallas_call | solution.py:449

commit v4 on v3

--- a/solution.py
+++ b/solution.py
@@ -34,9 +34,9 @@
 
 def kernel(
     scale,
-    qn_hbm, qr_hbm, wuk_hbm, wuv_hbm, cache_hbm, draft_hbm, pt_ref, len_ref, flags_ref,
+    qn_hbm, qr_hbm, wuk_hbm, wuv_hbm, cache_hbm, draft_hbm, pt_hbm, len_hbm, flags_hbm,
     out_ref, acc_ref, tot_ref,
-    qn, qr, wuk, wuv, pool, draft, kbuf, qbuf, nsend, nrecv, ssend, srecv,
+    pt_ref, len_ref, flags_ref, qn, qr, wuk, wuv, pool, draft, kbuf, qbuf, nsend, nrecv, ssend, srecv,
     csend, crecv, tsend, trecv, nd, md, ld, lo, count, counts,
     in_sem, key_s, key_r, q1_s, q1_r, q2_s, q2_r, n_s, n_r, s_s, s_r, c_s, c_r, t_s, t_r,
     a_s, a_r, far_sem,
@@ -53,6 +53,12 @@
     chip = lax.axis_index("kv_0") * RING + lax.axis_index("kv_1")
     partner = {"kv_2": 1 - core}
 
+    barrier = pltpu.get_barrier_semaphore()
+    near = [shifted(axis, by) for axis in ("kv_0", "kv_1", "seq") for by in (1, 3)]
+    peers = [partner] + near
+    for peer in peers:
+        pl.semaphore_signal(barrier, inc=1, device_id=peer, device_id_type=MESH)
+
     small = []
     for i, (src, dst) in enumerate(
         ((qn_hbm, qn), (wuk_hbm, wuk), (qr_hbm, qr), (draft_hbm, draft), (wuv_hbm, wuv))
@@ -67,28 +73,16 @@
         pools.append(pltpu.make_async_copy(cache_hbm.at[part], pool.at[part], in_sem.at[5 + i]))
         pools[-1].start()
     small[4].start()
-
-    barrier = pltpu.get_barrier_semaphore()
-    near = [shifted(axis, by) for axis in ("kv_0", "kv_1", "seq") for by in (1, 3)]
-    peers = [partner] + near
-    for peer in peers:
-        pl.semaphore_signal(barrier, inc=1, device_id=peer, device_id_type=MESH)
+    tables = []
+    for i, (src, dst) in enumerate(((pt_hbm, pt_ref), (len_hbm, len_ref), (flags_hbm, flags_ref))):
+        tables.append(pltpu.make_async_copy(src, dst, in_sem.at[9 + i]))
+        tables[-1].start()
 
     def remote(src, dst, send, recv, peer):
         return pltpu.make_async_remote_copy(
             src_ref=src, dst_ref=dst, send_sem=send, recv_sem=recv,
             device_id=peer, device_id_type=MESH,
         )
-
-    mine = jnp.int32(0)
-    for s in range(seqs):
-        run, total = jnp.int32(1), jnp.int32(0)
-        for i in range(flags_ref.shape[1]):
-            run = run * flags_ref[s, i]
-            total = total + run
-        acc_ref[s] = total
-        mine = mine + total
-    count[...] = jnp.full(count.shape, mine, jnp.int32)
 
     def arrived(dst, recv):
         remote(dst, dst, in_sem.at[0], recv, partner).wait_recv()
@@ -154,6 +148,9 @@
         for by in (1, 3):
             stage_two(h, 0, by)
 
+    for copy in tables:
+        copy.wait()
+
     for copy in pools:
         copy.wait()
     key_copies = []
@@ -190,6 +187,16 @@
         for by in (1, 3):
             stage_two(h, RING - by, by)
     send_keys(seqs - 1)
+
+    mine = jnp.int32(0)
+    for s in range(seqs):
+        run, total = jnp.int32(1), jnp.int32(0)
+        for i in range(flags_ref.shape[1]):
+            run = run * flags_ref[s, i]
+            total = total + run
+        acc_ref[s] = total
+        mine = mine + total
+    count[...] = jnp.full(count.shape, mine, jnp.int32)
 
     keys_d = draft[:, :latent]
     d_score = dot(q_lat, keys_d, NT) + dot(qr[...], draft[:, latent:], NT)
@@ -388,6 +395,9 @@
     vmem = pl.BlockSpec(memory_space=pltpu.VMEM)
     dma = pltpu.SemaphoreType.DMA
     scratch = [
+        pltpu.SMEM(page_table.shape, jnp.int32),
+        pltpu.SMEM(lengths.shape, jnp.int32),
+        pltpu.SMEM(flags.shape, jnp.int32),
         pltpu.VMEM((count, nope), bf16),
         pltpu.VMEM((count, rope), bf16),
         pltpu.VMEM(w_uk.shape, bf16),
@@ -410,7 +420,7 @@
         pltpu.VMEM((count, latent), bf16),
         pltpu.VMEM((8, 128), jnp.int32),
         pltpu.VMEM((RING - 1, 8, 128), jnp.int32),
-        dma((9,)),
+        dma((12,)),
         dma((seqs,)), dma((seqs,)),
         dma((2, 4)), dma((2, 4)),
         dma((2, RING - 1, RING)), dma((2, RING - 1, RING)),
@@ -428,7 +438,7 @@
             jax.ShapeDtypeStruct((seqs,), jnp.int32),
             jax.ShapeDtypeStruct((8, 128), jnp.int32),
         ),
-        in_specs=[hbm] * 6 + [smem] * 3,
+        in_specs=[hbm] * 9,
         out_specs=(vmem, smem, vmem),
         scratch_shapes=scratch,
         compiler_params=pltpu.CompilerParams(

time: 49.4 us -> 48.6 us (0.984)
  Pallas kernels: 48.5 us -> 47.8 us
    pallas_call x1, Pallas kernels: 47 us -> 46.3 us  [body(): pl.pallas_call(functools.partial(kernel, scale), out_shape=(jax.ShapeDtyp...]
where the time goes in v4:
time: 48.6 us; the launch traced here: 48.4 us
  Pallas kernels  47.8 us (98%)
  between operations  0.64 us (1%)
    pallas_call x1, Pallas kernels, body(): pl.pallas_call(functools.partial(kernel, scale), out_shape=(jax.ShapeDtyp...  46.3 us
    pallas_call x1, Pallas kernels, body(): pl.pallas_call(hand_over, out_shape=(jax.ShapeDtypeStruct(attended.shape,...  1.51 us

profile of v4, /device:TPU:0, one launch (start us, length us, event | category | flops | bytes accessed | tf_op | source)
XLA Modules:
  0.0 48.4 jit_solution(1726342653635062405)
XLA Ops:
  0.6 46.3 %verify.1 = (bf16[128,128]{1,0:T(8,128)(2,1)}, s32[4]{0:T(128)}, s32[8,128]{1,0:T(8,128)}) custom-call(bf16[128,128]{1,0:T(8,128)(2,1)} %bitcast.6, bf16[128,64]{1,0:T(8,128)(2,1)} %bitcast.7, bf16[4,128,512]{2,1,0:T(8,128)(2,1)} %wuk_hbm.1, bf16[4,512,128]{2,1,0:T(8,128)(2,1)} %wuv_hbm.1, bf16[64,64,576]{2,1,0:T(8,128)(2,1)} %cache_hbm.1, ...), custom_call_target="tpu_custom_call" | custom-call | tf_op jit(solution)/shard_map/verify/pallas_call | solution.py:434
  46.9 1.5 %hand_over.1 = (bf16[128,128]{1,0:T(8,128)(2,1)}, s32[4]{0:T(128)}, s32[1]{0:T(128)}) custom-call(bf16[128,128]{1,0:T(8,128)(2,1)} %get-tuple-element.9.a_ref, s32[4]{0:T(128)} %get-tuple-element.10.n_ref, s32[8,128]{1,0:T(8,128)} %get-tuple-element.11.t_ref), custom_call_target="tpu_custom_call" | custom-call | tf_op jit(solution)/shard_map/hand_over/pallas_call | solution.py:459

commit v5 on v4

--- a/solution.py
+++ b/solution.py
@@ -294,12 +294,16 @@
             for h in range(2):
                 if g == 0:
                     arrived(kbuf.at[2 * h + u, other], key_r.at[2 * h + u])
+            last = g == 1 and u == 1
             for h in range(2):
-                attend(h, u, group)
+                attend(h, u, (group[0], 1) if last else group)
             for h in range(2):
                 for place in range(group[0], group[0] + group[1]):
                     if place != HOME:
                         send_sums(h, u, place)
+            if last:
+                for h in range(2):
+                    attend(h, u, (HOME, 1))
 
     light = []
     for h, u in PAIRS:

time: 48.6 us -> 49.1 us (1.010)
  no operation moved by 1% of the time
where the time goes in v5:
time: 49.1 us; the launch traced here: 48.9 us
  Pallas kernels  48.1 us (98%)
  between operations  0.8 us (2%)
    pallas_call x1, Pallas kernels, body(): pl.pallas_call(functools.partial(kernel, scale), out_shape=(jax.ShapeDtyp...  46.6 us
    pallas_call x1, Pallas kernels, body(): pl.pallas_call(hand_over, out_shape=(jax.ShapeDtypeStruct(attended.shape,...  1.51 us

profile of v5, /device:TPU:0, one launch (start us, length us, event | category | flops | bytes accessed | tf_op | source)
XLA Modules:
  0.0 48.9 jit_solution(13655070622281957553)
XLA Ops:
  0.6 46.6 %verify.1 = (bf16[128,128]{1,0:T(8,128)(2,1)}, s32[4]{0:T(128)}, s32[8,128]{1,0:T(8,128)}) custom-call(bf16[128,128]{1,0:T(8,128)(2,1)} %bitcast.6, bf16[128,64]{1,0:T(8,128)(2,1)} %bitcast.7, bf16[4,128,512]{2,1,0:T(8,128)(2,1)} %wuk_hbm.1, bf16[4,512,128]{2,1,0:T(8,128)(2,1)} %wuv_hbm.1, bf16[64,64,576]{2,1,0:T(8,128)(2,1)} %cache_hbm.1, ...), custom_call_target="tpu_custom_call" | custom-call | tf_op jit(solution)/shard_map/verify/pallas_call | solution.py:438
  47.2 1.5 %hand_over.1 = (bf16[128,128]{1,0:T(8,128)(2,1)}, s32[4]{0:T(128)}, s32[1]{0:T(128)}) custom-call(bf16[128,128]{1,0:T(8,128)(2,1)} %get-tuple-element.9.a_ref, s32[4]{0:T(128)} %get-tuple-element.10.n_ref, s32[8,128]{1,0:T(8,128)} %get-tuple-element.11.t_ref), custom_call_target="tpu_custom_call" | custom-call | tf_op jit(solution)/shard_map/hand_over/pallas_call | solution.py:463
